TPU v7x, 32 devices: a whole 2x2x4 slice. The times are simulated.
32 devices in a mesh: row: 8 (over z, y), col: 4 (over x, core).
Axes of the slice: x: 2, y: 2, z: 4, core: 2. Of those that a mesh axis runs over, the one named last changes fastest.
Arguments:
- front: float32 [12, 8, 128, 24, 4, 128], P(None, 'row', None, None, 'col'), may hold values from -2.01 to 16, as said below
- child_updates: float32 [12, 8, 128, 12, 4, 128], P(None, 'row', None, None, 'col'), may hold values from -0.5 to 0.005, as said below
- child_maps: int32 [2, 48], replicated, may hold values from 0 to 62, as said below
- child_orders: int32 [2], replicated, may hold values from 6017 to 6144, as said below
Outputs:
- factored: float32 [12, 8, 128, 24, 4, 128], P(None, 'row', None, None, 'col')
Inputs may be any that keep to these rules, and one draw needn't show every extreme that they name: `front`: symmetric; with the children's updates added as above it is positive definite. `child_updates`: each child's update is symmetric. `child_maps`: each child's map adds to a tile's index an offset that is the same over aligned runs of 8 child tiles, rises strictly from run to run, is 0 on the first run and 15 on the last, and differs modulo 8 between runs. `child_orders`: each order lies in the last tile of its padded update; one of the two is 6144.
All inputs are finite; a program needn't handle non-finite values.
Results may differ from a plain program's by a relative error of at most 0.00005.
Values sent between devices are 32-bit elements; how exact they have to be, the bound alone decides.
A program may use at most 128 MiB of HBM per device.

v0:
```python
import jax
import jax.numpy as jnp
from jax import lax
from jax.sharding import PartitionSpec as P

PT = 5
PANELS = 1
RUN = 8


highest = lax.Precision.HIGHEST


def spread(value, axis, source):
    kept = jnp.where(lax.axis_index(axis) == source, value, 0).astype(value.dtype)
    return lax.psum(kept, axis)


def earlier_equal(values):
    length = values.shape[-1]
    matches = values[..., :, None] == values[..., None, :]
    earlier = jnp.arange(length)[None, :] < jnp.arange(length)[:, None]
    return jnp.sum(jnp.logical_and(matches, earlier), axis=-1)


def one_hot(values, length):
    return (values[..., None] == jnp.arange(length, dtype=jnp.int32)).astype(jnp.float32)


def shards(front, child_updates, child_maps, child_orders):
    row_tiles, tile_size, col_tiles = (front.shape[0], front.shape[2], front.shape[3])
    child_rows, child_cols = (child_updates.shape[0], child_updates.shape[3])
    rows_count = lax.axis_size("row")
    cols_count = lax.axis_size("col")
    half_rows = rows_count // 2
    group_size = rows_count // cols_count
    row_id = lax.axis_index("row")
    col_id = lax.axis_index("col")
    matrix = front.reshape(row_tiles, tile_size, col_tiles, tile_size)
    pieces = child_updates.reshape(child_rows, tile_size, child_cols, tile_size)
    cap_rows = max(1, 2 * RUN // rows_count)
    cap_cols = max(1, RUN // cols_count) ** 2
    sources = jnp.arange(rows_count, dtype=jnp.int32)
    source_child = sources // half_rows
    source_maps = jnp.where(
        source_child[:, None] == 0, child_maps[0][None, :], child_maps[1][None, :]
    )
    child_row_index = (
        jnp.arange(child_rows, dtype=jnp.int32)[None, :] * half_rows
        + (sources % half_rows)[:, None]
    )
    mapped_rows = jnp.take_along_axis(source_maps, child_row_index, axis=1)
    dest_rows = mapped_rows % rows_count
    slot_rows = mapped_rows // rows_count
    child_col_index = (
        jnp.arange(child_cols, dtype=jnp.int32)[None, :] * cols_count
        + jnp.arange(cols_count, dtype=jnp.int32)[:, None]
    )
    mapped_cols = child_maps[:, child_col_index]
    dest_cols = mapped_cols % cols_count
    slot_cols = mapped_cols // cols_count
    my_child = row_id // half_rows
    my_order = jnp.where(my_child == 0, child_orders[0], child_orders[1])
    my_rows = child_row_index[row_id]
    my_cols = jnp.arange(child_cols, dtype=jnp.int32) * cols_count + col_id
    offsets = jnp.arange(tile_size, dtype=jnp.int32)[None, :]
    row_keep = (my_rows[:, None] * tile_size + offsets < my_order).astype(jnp.float32)
    col_keep = (my_cols[:, None] * tile_size + offsets < my_order).astype(jnp.float32)
    pieces = pieces * row_keep[:, :, None, None] * col_keep[None, None, :, :]
    capacity = cap_rows * cap_cols
    tile_count = child_rows * child_cols
    source_dest_cols = dest_cols[source_child]
    source_slot_cols = slot_cols[source_child]
    tile_dest = (
        dest_rows[:, None, :, None] * cols_count + source_dest_cols[:, :, None, :]
    ).reshape(rows_count, cols_count, tile_count)
    rank_tiles = earlier_equal(tile_dest)
    send_tiles = (
        one_hot(tile_dest[row_id, col_id], rows_count * cols_count)[:, :, None]
        * one_hot(rank_tiles[row_id, col_id], capacity)[:, None, :]
    )
    flat_pieces = pieces.transpose(0, 2, 1, 3).reshape(tile_count, tile_size, tile_size)
    outgoing = jnp.einsum("fpq,frs->pqrs", send_tiles, flat_pieces, precision=highest)
    incoming = lax.all_to_all(outgoing, ("row", "col"), split_axis=0, concat_axis=0, tiled=True)
    arrive_tiles = (tile_dest == row_id * cols_count + col_id).astype(jnp.float32)
    row_slot_flat = jnp.broadcast_to(
        slot_rows[:, None, :, None], (rows_count, cols_count, child_rows, child_cols)
    ).reshape(rows_count, cols_count, tile_count)
    col_slot_flat = jnp.broadcast_to(
        source_slot_cols[:, :, None, :], (rows_count, cols_count, child_rows, child_cols)
    ).reshape(rows_count, cols_count, tile_count)
    placement = jnp.einsum(
        "jlf,jlfa,jlfb,jlfq->abjlq",
        arrive_tiles,
        one_hot(row_slot_flat, row_tiles),
        one_hot(col_slot_flat, col_tiles),
        one_hot(rank_tiles, capacity),
        precision=highest,
    )
    placement = placement.reshape(row_tiles, col_tiles, rows_count * cols_count, capacity)
    added = jnp.einsum("abpq,pqrs->arbs", placement, incoming, precision=highest)
    matrix = matrix + added
    glob_rows = jnp.arange(row_tiles, dtype=jnp.int32) * rows_count + row_id
    glob_cols = jnp.arange(col_tiles, dtype=jnp.int32) * cols_count + col_id
    identity = jnp.eye(tile_size, dtype=jnp.float32)

    def factor_column(matrix, column_tile):
        owner_col = column_tile % cols_count
        local_col = column_tile // cols_count
        owner_row = column_tile % rows_count
        local_row = column_tile // rows_count
        column = lax.dynamic_index_in_dim(matrix, local_col, 2, keepdims=False)
        pivot_local = lax.dynamic_index_in_dim(column, local_row, 0, keepdims=False)
        pivot_local = jnp.where(col_id == owner_col, pivot_local, identity)
        pivot = spread(pivot_local, "row", owner_row)
        factor = jnp.tril(jnp.linalg.cholesky(pivot))
        solved = lax.linalg.triangular_solve(
            factor,
            column.reshape(row_tiles * tile_size, tile_size),
            left_side=False,
            lower=True,
            transpose_a=True,
        ).reshape(row_tiles, tile_size, tile_size)
        below = (glob_rows > column_tile)[:, None, None]
        diagonal = (glob_rows == column_tile)[:, None, None]
        panel_part = jnp.where(below, solved, jnp.where(diagonal, factor[None], 0.0))
        lower_rows = spread(panel_part, "col", owner_col)
        received = []
        for member in range(group_size):
            received.append(spread(lower_rows, "row", col_id + member * cols_count))
        lower_cols = jnp.stack(received, 1).reshape(col_tiles, tile_size, tile_size)
        new_column = jnp.where(col_id == owner_col, panel_part, column)
        matrix = lax.dynamic_update_index_in_dim(matrix, new_column, local_col, 2)
        lower_rows = jnp.where(below, lower_rows, 0.0)
        lower_cols = jnp.where((glob_cols > column_tile)[:, None, None], lower_cols, 0.0)
        return (matrix, lower_rows, lower_cols)

    def column_turn(column, matrix):
        matrix, lower_rows, lower_cols = factor_column(matrix, 0 + column)
        return matrix - jnp.einsum("trx,usx->trus", lower_rows, lower_cols, precision=highest)

    matrix = lax.fori_loop(0, PT, column_turn, matrix)
    factored_tiles = PANELS * PT
    upper_block = jnp.logical_and(
        (glob_rows < factored_tiles)[:, None], (glob_cols >= factored_tiles)[None, :]
    )
    matrix = jnp.where(upper_block[:, None, :, None], 0.0, matrix)
    return matrix.reshape(row_tiles, 1, tile_size, col_tiles, 1, tile_size)


def solution(mesh):
    in_specs = (
        P(None, "row", None, None, "col", None),
        P(None, "row", None, None, "col", None),
        P(),
        P(),
    )
    out_specs = P(None, "row", None, None, "col", None)
    return jax.shard_map(shards, mesh=mesh, in_specs=in_specs, out_specs=out_specs, check_vma=False)
```

profile of v0, /device:TPU:0, one launch (start us, length us, event | category | flops | bytes accessed | tf_op | source)
XLA Modules:
  0.0 1745.6 jit_solution(7277346975675810042)
XLA Ops:
  21.2 24.4 %fusion.22 = f32[32,8,128,128]{3,1,2,0:T(8,128)} fusion(f32[144,128,128]{2,1,0:T(8,128)S(1)} %bitcast.144, f32[144,32,8,1]{0,1,2,3:T(8,128)S(1)} %multiply_bitcast_fusion), kind=kOutput, calls=%fused_computation.45 | convolution fusion | flops 7247757312 | bytes 26361856 | tf_op jit(solution)/shard_map/fpq,frs->pqrs/dot_general | solution.py:83
  56.7 369.1 %all-to-all-done = f32[32,8,128,128]{3,1,2,0:T(8,128)} async-done(((f32[32,8,128,128]{3,1,2,0:T(8,128)}), f32[32,8,128,128]{3,1,2,0:T(8,128)}, u32[]{:S(2)}, u32[]{:S(2)}) %all-to-all-start) | async-done | bytes 16777248 | tf_op jit(solution)/shard_map/all_to_all | solution.py:84
  425.8 29.5 %bitcast_add_fusion.1 = f32[12,128,24,128]{3,2,0,1:T(8,128)} fusion(f32[12,1,128,24,1,128]{5,4,3,2,1,0:T(1,128)} %param.6, f32[12,24,32,8]{1,0,3,2:T(8,128)S(1)} %bitcast.145, f32[32,8,128,128]{3,1,2,0:T(8,128)} %all-to-all-done), kind=kOutput, calls=%fused_computation.41 | convolution fusion | flops 14500233216 | bytes 54820864 | tf_op jit(solution)/shard_map/abpq,pqrs->arbs/dot_general | solution.py:101
  455.2 15.6 copy.69
  470.8 1247.6 %while.18 = (s32[]{:T(128)}, f32[12,128,24,128]{3,1,2,0:T(8,128)}, s32[]{:T(128)}, s32[]{:T(128)}, s32[]{:T(128)}, /*index=5*/s32[]{:T(128)}, s32[]{:T(128)}, s3...) while((s32[]{:T(128)}, f32[12,128,24,128]{3,1,2,0:T(8,128)}, ...), condition=%wide.region_8.9_spmd.clone.clone, body=%wide.region_1.8_spmd.clone.clone.sunk | while | flops 7557464576 | bytes 76744584 | solution.py:142
  472.7 67.7 %all-reduce.7.cloned.1.call-done = f32[128,128]{1,0:T(8,128)} async-done(((f32[128,128]{1,0:T(8,128)}), f32[128,128]{1,0:T(8,128)}) %all-reduce.7.cloned.1.call-update) | async-done | bytes 65552 | tf_op jit(solution)/shard_map/while/body/eval_jaxpr/psum | solution.py:16
  542.2 11.7 cholesky.69
  555.3 9.8 custom-call.33
  568.0 35.1 %all-reduce.9.cloned.1.call-done = f32[12,128,128]{2,1,0:T(8,128)} async-done(((f32[12,128,128]{2,1,0:T(8,128)}), f32[12,128,128]{2,1,0:T(8,128)}) %all-reduce.9.cloned.1.call-update) | async-done | bytes 786448 | tf_op jit(solution)/shard_map/while/body/eval_jaxpr/psum | solution.py:16
  607.8 88.2 %all-reduce.11.cloned.1.call-done = (f32[12,1,128,128]{3,2,0,1:T(8,128)}, f32[12,1,128,128]{3,2,0,1:T(8,128)}) async-done(((f32[12,1,128,128]{3,2,0,1:T(8,128)}, f32[12,1,128,128]{3,2,0,1:T(8,128)}), (f32[12,1,128,128]{3,2,0,1:T(8,128)}, f32[12,1,128,128]{3,2,0,1:T(8,128)})) %all-reduce.11.cloned.1.call-update) | async-done | bytes 1572880 | tf_op jit(solution)/shard_map/while/body/eval_jaxpr/psum | solution.py:16
  697.8 20.3 %convolution_subtract_fusion.2 = f32[12,128,24,128]{3,1,2,0:T(8,128)} fusion(f32[12,128,24,128]{3,1,2,0:T(8,128)} %bitcast_dynamic-update-slice_fusion.2, f32[24,128,128]{2,1,0:T(8,128)S(1)} %bitcast_select_fusion.4, f32[12,128,128]{2,1,0:T(8,128)S(1)} %copy-done, pred[12]{0:T(512)(128)(4,1)S(1)} %get-tuple-element.344), kind=kOutput, calls=%fused_computation.7.clone.1 | convolution fusion | flops 7252672512 | bytes 40108044 | tf_op jit(solution)/shard_map/while/body/eval_jaxpr/trx,usx->trus/dot_general | solution.py:140
  719.7 70.8 %all-reduce.7.cloned.1.call-done = f32[128,128]{1,0:T(8,128)} async-done(((f32[128,128]{1,0:T(8,128)}), f32[128,128]{1,0:T(8,128)}) %all-reduce.7.cloned.1.call-update) | async-done | bytes 65552 | tf_op jit(solution)/shard_map/while/body/eval_jaxpr/psum | solution.py:16
  792.3 11.7 cholesky.69
  818.0 35.1 %all-reduce.9.cloned.1.call-done = f32[12,128,128]{2,1,0:T(8,128)} async-done(((f32[12,128,128]{2,1,0:T(8,128)}), f32[12,128,128]{2,1,0:T(8,128)}) %all-reduce.9.cloned.1.call-update) | async-done | bytes 786448 | tf_op jit(solution)/shard_map/while/body/eval_jaxpr/psum | solution.py:16
  857.9 88.0 %all-reduce.11.cloned.1.call-done = (f32[12,1,128,128]{3,2,0,1:T(8,128)}, f32[12,1,128,128]{3,2,0,1:T(8,128)}) async-done(((f32[12,1,128,128]{3,2,0,1:T(8,128)}, f32[12,1,128,128]{3,2,0,1:T(8,128)}), (f32[12,1,128,128]{3,2,0,1:T(8,128)}, f32[12,1,128,128]{3,2,0,1:T(8,128)})) %all-reduce.11.cloned.1.call-update) | async-done | bytes 1572880 | tf_op jit(solution)/shard_map/while/body/eval_jaxpr/psum | solution.py:16
  947.7 20.3 %convolution_subtract_fusion.2 = f32[12,128,24,128]{3,1,2,0:T(8,128)} fusion(f32[12,128,24,128]{3,1,2,0:T(8,128)} %bitcast_dynamic-update-slice_fusion.2, f32[24,128,128]{2,1,0:T(8,128)S(1)} %bitcast_select_fusion.4, f32[12,128,128]{2,1,0:T(8,128)S(1)} %copy-done, pred[12]{0:T(512)(128)(4,1)S(1)} %get-tuple-element.344), kind=kOutput, calls=%fused_computation.7.clone.1 | convolution fusion | flops 7252672512 | bytes 40108044 | tf_op jit(solution)/shard_map/while/body/eval_jaxpr/trx,usx->trus/dot_general | solution.py:140
  969.6 71.1 %all-reduce.7.cloned.1.call-done = f32[128,128]{1,0:T(8,128)} async-done(((f32[128,128]{1,0:T(8,128)}), f32[128,128]{1,0:T(8,128)}) %all-reduce.7.cloned.1.call-update) | async-done | bytes 65552 | tf_op jit(solution)/shard_map/while/body/eval_jaxpr/psum | solution.py:16
  1042.5 11.7 cholesky.69
  1068.3 35.0 %all-reduce.9.cloned.1.call-done = f32[12,128,128]{2,1,0:T(8,128)} async-done(((f32[12,128,128]{2,1,0:T(8,128)}), f32[12,128,128]{2,1,0:T(8,128)}) %all-reduce.9.cloned.1.call-update) | async-done | bytes 786448 | tf_op jit(solution)/shard_map/while/body/eval_jaxpr/psum | solution.py:16
  1108.1 88.2 %all-reduce.11.cloned.1.call-done = (f32[12,1,128,128]{3,2,0,1:T(8,128)}, f32[12,1,128,128]{3,2,0,1:T(8,128)}) async-done(((f32[12,1,128,128]{3,2,0,1:T(8,128)}, f32[12,1,128,128]{3,2,0,1:T(8,128)}), (f32[12,1,128,128]{3,2,0,1:T(8,128)}, f32[12,1,128,128]{3,2,0,1:T(8,128)})) %all-reduce.11.cloned.1.call-update) | async-done | bytes 1572880 | tf_op jit(solution)/shard_map/while/body/eval_jaxpr/psum | solution.py:16
  1198.0 20.3 %convolution_subtract_fusion.2 = f32[12,128,24,128]{3,1,2,0:T(8,128)} fusion(f32[12,128,24,128]{3,1,2,0:T(8,128)} %bitcast_dynamic-update-slice_fusion.2, f32[24,128,128]{2,1,0:T(8,128)S(1)} %bitcast_select_fusion.4, f32[12,128,128]{2,1,0:T(8,128)S(1)} %copy-done, pred[12]{0:T(512)(128)(4,1)S(1)} %get-tuple-element.344), kind=kOutput, calls=%fused_computation.7.clone.1 | convolution fusion | flops 7252672512 | bytes 40108044 | tf_op jit(solution)/shard_map/while/body/eval_jaxpr/trx,usx->trus/dot_general | solution.py:140
  1220.0 70.8 %all-reduce.7.cloned.1.call-done = f32[128,128]{1,0:T(8,128)} async-done(((f32[128,128]{1,0:T(8,128)}), f32[128,128]{1,0:T(8,128)}) %all-reduce.7.cloned.1.call-update) | async-done | bytes 65552 | tf_op jit(solution)/shard_map/while/body/eval_jaxpr/psum | solution.py:16
  1292.6 11.7 cholesky.69
  1318.3 35.0 %all-reduce.9.cloned.1.call-done = f32[12,128,128]{2,1,0:T(8,128)} async-done(((f32[12,128,128]{2,1,0:T(8,128)}), f32[12,128,128]{2,1,0:T(8,128)}) %all-reduce.9.cloned.1.call-update) | async-done | bytes 786448 | tf_op jit(solution)/shard_map/while/body/eval_jaxpr/psum | solution.py:16
  1358.1 88.0 %all-reduce.11.cloned.1.call-done = (f32[12,1,128,128]{3,2,0,1:T(8,128)}, f32[12,1,128,128]{3,2,0,1:T(8,128)}) async-done(((f32[12,1,128,128]{3,2,0,1:T(8,128)}, f32[12,1,128,128]{3,2,0,1:T(8,128)}), (f32[12,1,128,128]{3,2,0,1:T(8,128)}, f32[12,1,128,128]{3,2,0,1:T(8,128)})) %all-reduce.11.cloned.1.call-update) | async-done | bytes 1572880 | tf_op jit(solution)/shard_map/while/body/eval_jaxpr/psum | solution.py:16
  1447.9 20.3 %convolution_subtract_fusion.2 = f32[12,128,24,128]{3,1,2,0:T(8,128)} fusion(f32[12,128,24,128]{3,1,2,0:T(8,128)} %bitcast_dynamic-update-slice_fusion.2, f32[24,128,128]{2,1,0:T(8,128)S(1)} %bitcast_select_fusion.4, f32[12,128,128]{2,1,0:T(8,128)S(1)} %copy-done, pred[12]{0:T(512)(128)(4,1)S(1)} %get-tuple-element.344), kind=kOutput, calls=%fused_computation.7.clone.1 | convolution fusion | flops 7252672512 | bytes 40108044 | tf_op jit(solution)/shard_map/while/body/eval_jaxpr/trx,usx->trus/dot_general | solution.py:140
  1469.9 71.1 %all-reduce.7.cloned.1.call-done = f32[128,128]{1,0:T(8,128)} async-done(((f32[128,128]{1,0:T(8,128)}), f32[128,128]{1,0:T(8,128)}) %all-reduce.7.cloned.1.call-update) | async-done | bytes 65552 | tf_op jit(solution)/shard_map/while/body/eval_jaxpr/psum | solution.py:16
  1542.8 11.7 cholesky.69
  1568.5 35.0 %all-reduce.9.cloned.1.call-done = f32[12,128,128]{2,1,0:T(8,128)} async-done(((f32[12,128,128]{2,1,0:T(8,128)}), f32[12,128,128]{2,1,0:T(8,128)}) %all-reduce.9.cloned.1.call-update) | async-done | bytes 786448 | tf_op jit(solution)/shard_map/while/body/eval_jaxpr/psum | solution.py:16
  1608.3 88.0 %all-reduce.11.cloned.1.call-done = (f32[12,1,128,128]{3,2,0,1:T(8,128)}, f32[12,1,128,128]{3,2,0,1:T(8,128)}) async-done(((f32[12,1,128,128]{3,2,0,1:T(8,128)}, f32[12,1,128,128]{3,2,0,1:T(8,128)}), (f32[12,1,128,128]{3,2,0,1:T(8,128)}, f32[12,1,128,128]{3,2,0,1:T(8,128)})) %all-reduce.11.cloned.1.call-update) | async-done | bytes 1572880 | tf_op jit(solution)/shard_map/while/body/eval_jaxpr/psum | solution.py:16
  1698.1 20.3 %convolution_subtract_fusion.2 = f32[12,128,24,128]{3,1,2,0:T(8,128)} fusion(f32[12,128,24,128]{3,1,2,0:T(8,128)} %bitcast_dynamic-update-slice_fusion.2, f32[24,128,128]{2,1,0:T(8,128)S(1)} %bitcast_select_fusion.4, f32[12,128,128]{2,1,0:T(8,128)S(1)} %copy-done, pred[12]{0:T(512)(128)(4,1)S(1)} %get-tuple-element.344), kind=kOutput, calls=%fused_computation.7.clone.1 | convolution fusion | flops 7252672512 | bytes 40108044 | tf_op jit(solution)/shard_map/while/body/eval_jaxpr/trx,usx->trus/dot_general | solution.py:140
  1718.5 20.1 %copy_select_fusion = f32[12,128,24,128]{3,2,1,0:T(8,128)} fusion(f32[12,128,24,128]{3,1,2,0:T(8,128)} %get-tuple-element.212, pred[12,24]{1,0:T(8,128)(4,1)S(1)} %broadcast_and_fusion), kind=kLoop, calls=%fused_computation.42 | loop fusion | flops 4718592 | bytes 37749024 | tf_op jit(solution)/shard_map/jit(_where)/select_n | solution.py:147
  (174 shorter events, 133.5 us)
Async XLA Ops:
  45.6 380.2 %all-to-all-start = ((f32[32,8,128,128]{3,1,2,0:T(8,128)}), f32[32,8,128,128]{3,1,2,0:T(8,128)}, u32[]{:S(2)}, u32[]{:S(2)}) async-start(f32[32,8,128,128]{3,1,2,0:T(8,128)} %fusion.22), calls=%async_computation | async-start | bytes 33554432 | tf_op jit(solution)/shard_map/all_to_all | solution.py:84
  471.0 69.4 %all-reduce.7.cloned.1.call-start = ((), (), s32[]{:S(2)}) async-start(), calls=%async_computation.1 | async-start | bytes 131072 | tf_op jit(solution)/shard_map/while/body/eval_jaxpr/psum | solution.py:16
  472.7 130.4 %all-reduce.9.cloned.1.call-start = ((), (), s32[]{:S(2)}) async-start(), calls=%async_computation.2 | async-start | bytes 1572864 | tf_op jit(solution)/shard_map/while/body/eval_jaxpr/psum | solution.py:16
  567.9 128.1 %all-reduce.11.cloned.1.call-start = ((), (), s32[]{:S(2)}) async-start(), calls=%async_computation.3 | async-start | bytes 3145728 | tf_op jit(solution)/shard_map/while/body/eval_jaxpr/psum | solution.py:16
  603.1 94.7 %copy-start = (f32[12,128,128]{2,1,0:T(8,128)S(1)}, f32[12,128,128]{2,1,0:T(8,128)}, u32[]{:S(2)}) copy-start(f32[12,128,128]{2,1,0:T(8,128)} %all-reduce.9.cloned.1.call-done) | copy-start | bytes 2359300 | tf_op jit(solution)/shard_map/while
  718.1 72.4 %all-reduce.7.cloned.1.call-start = ((), (), s32[]{:S(2)}) async-start(), calls=%async_computation.1 | async-start | bytes 131072 | tf_op jit(solution)/shard_map/while/body/eval_jaxpr/psum | solution.py:16
  719.6 133.5 %all-reduce.9.cloned.1.call-start = ((), (), s32[]{:S(2)}) async-start(), calls=%async_computation.2 | async-start | bytes 1572864 | tf_op jit(solution)/shard_map/while/body/eval_jaxpr/psum | solution.py:16
  818.0 127.9 %all-reduce.11.cloned.1.call-start = ((), (), s32[]{:S(2)}) async-start(), calls=%async_computation.3 | async-start | bytes 3145728 | tf_op jit(solution)/shard_map/while/body/eval_jaxpr/psum | solution.py:16
  853.1 94.6 %copy-start = (f32[12,128,128]{2,1,0:T(8,128)S(1)}, f32[12,128,128]{2,1,0:T(8,128)}, u32[]{:S(2)}) copy-start(f32[12,128,128]{2,1,0:T(8,128)} %all-reduce.9.cloned.1.call-done) | copy-start | bytes 2359300 | tf_op jit(solution)/shard_map/while
  968.0 72.7 %all-reduce.7.cloned.1.call-start = ((), (), s32[]{:S(2)}) async-start(), calls=%async_computation.1 | async-start | bytes 131072 | tf_op jit(solution)/shard_map/while/body/eval_jaxpr/psum | solution.py:16
  969.5 133.8 %all-reduce.9.cloned.1.call-start = ((), (), s32[]{:S(2)}) async-start(), calls=%async_computation.2 | async-start | bytes 1572864 | tf_op jit(solution)/shard_map/while/body/eval_jaxpr/psum | solution.py:16
  1068.2 128.0 %all-reduce.11.cloned.1.call-start = ((), (), s32[]{:S(2)}) async-start(), calls=%async_computation.3 | async-start | bytes 3145728 | tf_op jit(solution)/shard_map/while/body/eval_jaxpr/psum | solution.py:16
  1103.3 94.7 %copy-start = (f32[12,128,128]{2,1,0:T(8,128)S(1)}, f32[12,128,128]{2,1,0:T(8,128)}, u32[]{:S(2)}) copy-start(f32[12,128,128]{2,1,0:T(8,128)} %all-reduce.9.cloned.1.call-done) | copy-start | bytes 2359300 | tf_op jit(solution)/shard_map/while
  1218.4 72.4 %all-reduce.7.cloned.1.call-start = ((), (), s32[]{:S(2)}) async-start(), calls=%async_computation.1 | async-start | bytes 131072 | tf_op jit(solution)/shard_map/while/body/eval_jaxpr/psum | solution.py:16
  1219.9 133.5 %all-reduce.9.cloned.1.call-start = ((), (), s32[]{:S(2)}) async-start(), calls=%async_computation.2 | async-start | bytes 1572864 | tf_op jit(solution)/shard_map/while/body/eval_jaxpr/psum | solution.py:16
  1318.3 127.9 %all-reduce.11.cloned.1.call-start = ((), (), s32[]{:S(2)}) async-start(), calls=%async_computation.3 | async-start | bytes 3145728 | tf_op jit(solution)/shard_map/while/body/eval_jaxpr/psum | solution.py:16
  1353.4 94.6 %copy-start = (f32[12,128,128]{2,1,0:T(8,128)S(1)}, f32[12,128,128]{2,1,0:T(8,128)}, u32[]{:S(2)}) copy-start(f32[12,128,128]{2,1,0:T(8,128)} %all-reduce.9.cloned.1.call-done) | copy-start | bytes 2359300 | tf_op jit(solution)/shard_map/while
  1468.3 72.7 %all-reduce.7.cloned.1.call-start = ((), (), s32[]{:S(2)}) async-start(), calls=%async_computation.1 | async-start | bytes 131072 | tf_op jit(solution)/shard_map/while/body/eval_jaxpr/psum | solution.py:16
  1469.8 133.8 %all-reduce.9.cloned.1.call-start = ((), (), s32[]{:S(2)}) async-start(), calls=%async_computation.2 | async-start | bytes 1572864 | tf_op jit(solution)/shard_map/while/body/eval_jaxpr/psum | solution.py:16
  1568.5 127.9 %all-reduce.11.cloned.1.call-start = ((), (), s32[]{:S(2)}) async-start(), calls=%async_computation.3 | async-start | bytes 3145728 | tf_op jit(solution)/shard_map/while/body/eval_jaxpr/psum | solution.py:16
  1603.6 94.5 %copy-start = (f32[12,128,128]{2,1,0:T(8,128)S(1)}, f32[12,128,128]{2,1,0:T(8,128)}, u32[]{:S(2)}) copy-start(f32[12,128,128]{2,1,0:T(8,128)} %all-reduce.9.cloned.1.call-done) | copy-start | bytes 2359300 | tf_op jit(solution)/shard_map/while
Sparse Core Ops, SparseCore 0:
  475.3 65.1 all-reduce.6
  568.0 34.9 all-reduce.8
  606.6 89.3 all-reduce.10
  722.0 68.4 all-reduce.6
  818.1 34.9 all-reduce.8
  856.6 89.3 all-reduce.10
  972.2 68.4 all-reduce.6
  1068.3 34.9 all-reduce.8
  1106.9 89.3 all-reduce.10
  1222.3 68.4 all-reduce.6
  1318.4 34.9 all-reduce.8
  1356.8 89.3 all-reduce.10
  1472.5 68.4 all-reduce.6
  1568.6 34.9 all-reduce.8
  1607.0 89.3 all-reduce.10
where the time goes:
time: 1750 us
  waiting for transfers between devices  1340 us (77%)
  other arithmetic  180 us (10%)
  matrix products  172 us (10%)
  local copies, waits for them, and re-layouts  33.4 us (2%)
    psum x15, waiting for transfers between devices, spread(): return lax.psum(kept, axis)  967 us
    all_to_all x1, waiting for transfers between devices, shards(): lax.all_to_all(outgoing, ('row', 'col'), split_axis=0, concat_axis=0, til...  369 us
    dot_general x5, matrix products, column_turn(): jnp.einsum('trx,usx->trus', lower_rows, lower_cols, precision=highest)  102 us
    another operation x15, other arithmetic, factor_column(): factor = jnp.tril(jnp.linalg.cholesky(pivot))  61.9 us
    another operation x10, other arithmetic, factor_column(): lax.linalg.triangular_solve(factor, column.reshape(row_tiles * tile_size,...  52.3 us
  transfers between devices with their start and end apart: 16, of which 16 were waited for; matrix products, arithmetic and copies ran while one was open for 1% of the time, Pallas kernels for 0%

commit v1 on v0

--- a/solution.py
+++ b/solution.py
@@ -9,11 +9,6 @@
 
 
 highest = lax.Precision.HIGHEST
-
-
-def spread(value, axis, source):
-    kept = jnp.where(lax.axis_index(axis) == source, value, 0).astype(value.dtype)
-    return lax.psum(kept, axis)
 
 
 def earlier_equal(values):
@@ -33,7 +28,6 @@
     rows_count = lax.axis_size("row")
     cols_count = lax.axis_size("col")
     half_rows = rows_count // 2
-    group_size = rows_count // cols_count
     row_id = lax.axis_index("row")
     col_id = lax.axis_index("col")
     matrix = front.reshape(row_tiles, tile_size, col_tiles, tile_size)
@@ -101,50 +95,46 @@
     added = jnp.einsum("abpq,pqrs->arbs", placement, incoming, precision=highest)
     matrix = matrix + added
     glob_rows = jnp.arange(row_tiles, dtype=jnp.int32) * rows_count + row_id
-    glob_cols = jnp.arange(col_tiles, dtype=jnp.int32) * cols_count + col_id
-    identity = jnp.eye(tile_size, dtype=jnp.float32)
 
-    def factor_column(matrix, column_tile):
-        owner_col = column_tile % cols_count
-        local_col = column_tile // cols_count
-        owner_row = column_tile % rows_count
-        local_row = column_tile // rows_count
-        column = lax.dynamic_index_in_dim(matrix, local_col, 2, keepdims=False)
-        pivot_local = lax.dynamic_index_in_dim(column, local_row, 0, keepdims=False)
-        pivot_local = jnp.where(col_id == owner_col, pivot_local, identity)
-        pivot = spread(pivot_local, "row", owner_row)
-        factor = jnp.tril(jnp.linalg.cholesky(pivot))
-        solved = lax.linalg.triangular_solve(
-            factor,
-            column.reshape(row_tiles * tile_size, tile_size),
-            left_side=False,
-            lower=True,
-            transpose_a=True,
-        ).reshape(row_tiles, tile_size, tile_size)
-        below = (glob_rows > column_tile)[:, None, None]
-        diagonal = (glob_rows == column_tile)[:, None, None]
-        panel_part = jnp.where(below, solved, jnp.where(diagonal, factor[None], 0.0))
-        lower_rows = spread(panel_part, "col", owner_col)
-        received = []
-        for member in range(group_size):
-            received.append(spread(lower_rows, "row", col_id + member * cols_count))
-        lower_cols = jnp.stack(received, 1).reshape(col_tiles, tile_size, tile_size)
-        new_column = jnp.where(col_id == owner_col, panel_part, column)
-        matrix = lax.dynamic_update_index_in_dim(matrix, new_column, local_col, 2)
-        lower_rows = jnp.where(below, lower_rows, 0.0)
-        lower_cols = jnp.where((glob_cols > column_tile)[:, None, None], lower_cols, 0.0)
-        return (matrix, lower_rows, lower_cols)
-
-    def column_turn(column, matrix):
-        matrix, lower_rows, lower_cols = factor_column(matrix, 0 + column)
-        return matrix - jnp.einsum("trx,usx->trus", lower_rows, lower_cols, precision=highest)
-
-    matrix = lax.fori_loop(0, PT, column_turn, matrix)
-    factored_tiles = PANELS * PT
-    upper_block = jnp.logical_and(
-        (glob_rows < factored_tiles)[:, None], (glob_cols >= factored_tiles)[None, :]
+    panel_tiles = PANELS * PT
+    panel_order = panel_tiles * tile_size
+    lead_cols = -(-panel_tiles // cols_count)
+    high = lax.Precision.HIGH
+    panel_rows = lax.all_gather(matrix[:, :, :lead_cols, :], "col", axis=3)
+    panel_rows = panel_rows.reshape(row_tiles * tile_size, lead_cols * cols_count * tile_size)
+    panel_rows = panel_rows[:, :panel_order]
+    leading = lax.all_gather(panel_rows[:tile_size], "row", axis=0)[:panel_tiles]
+    leading = leading.reshape(panel_order, panel_order)
+    panel_cols = lax.all_gather(matrix[0], "row", axis=0)[:panel_tiles]
+    panel_cols = panel_cols.reshape(panel_order, col_tiles * tile_size)
+    factor = jnp.tril(jnp.linalg.cholesky(leading))
+    inverse = lax.linalg.triangular_solve(
+        factor, jnp.eye(panel_order, dtype=jnp.float32), left_side=True, lower=True
     )
-    matrix = jnp.where(upper_block[:, None, :, None], 0.0, matrix)
+    lower_rows = jnp.einsum("rx,yx->ry", panel_rows, inverse, precision=high)
+    lower_cols = jnp.einsum("yx,xc->yc", inverse, panel_cols, precision=high)
+    below = (glob_rows >= panel_tiles)[:, None, None]
+    lower_tiles = jnp.where(below, lower_rows.reshape(row_tiles, tile_size, panel_order), 0.0)
+    update = jnp.einsum(
+        "trx,xus->trus",
+        lower_tiles,
+        lower_cols.reshape(panel_order, col_tiles, tile_size),
+        precision=high,
+    )
+    matrix = jnp.where(below[..., None], matrix - update, 0.0)
+    factor_row = lax.dynamic_slice_in_dim(
+        factor, jnp.minimum(row_id, panel_tiles - 1) * tile_size, tile_size, 0
+    )
+    top = jnp.where(row_id < panel_tiles, factor_row, lower_tiles[0])
+    panel = jnp.concatenate([top[None], lower_tiles[1:]], 0)
+    for local_col in range(lead_cols):
+        column = local_col * cols_count + col_id
+        piece = lax.dynamic_slice_in_dim(
+            panel, jnp.minimum(column, panel_tiles - 1) * tile_size, tile_size, 2
+        )
+        matrix = matrix.at[:, :, local_col, :].set(
+            jnp.where(column < panel_tiles, piece, matrix[:, :, local_col, :])
+        )
     return matrix.reshape(row_tiles, 1, tile_size, col_tiles, 1, tile_size)
 
 

time: 1750 us -> 918 us (0.52)
  waiting for transfers between devices: 1340 us -> 464 us
  local copies, waits for them, and re-layouts: 33.4 us -> 107 us
  matrix products: 172 us -> 113 us
    psum x15 -> x0, waiting for transfers between devices: 967 us -> none  [spread(): return lax.psum(kept, axis)]
    all_gather x0 -> x3, waiting for transfers between devices: none -> 94.9 us  [the longest x1 52.2 us: shards(): lax.all_gather(panel_rows[:tile_size], 'row', axis=0)[:panel_tiles]]
    dot_general x5 -> x3, matrix products: 102 us -> 47.8 us  [the longest x1 28.4 us: shards(): jnp.einsum('trx,xus->trus', lower_tiles, lower_cols.reshape(panel_order,...]
    another operation x37 -> x24, other arithmetic: 134 us -> 164 us  [the longest x19 110 us: shards(): factor = jnp.tril(jnp.linalg.cholesky(leading))]
    select_n x11 -> x1, other arithmetic: 28.4 us -> 0.41 us  [shards(): jnp.where(below, lower_rows.reshape(row_tiles, tile_size, panel_order), 0.0)]
    scatter x0 -> x1, local copies, waits for them, and re-layouts: none -> 22.5 us  [shards(): matrix.at[:, :, local_col, :]]
    add x0 -> x1, other arithmetic: none -> 18.5 us  [shards(): matrix = matrix + added]
    another operation x6 -> x22, local copies, waits for them, and re-layouts: 0.53 us -> 18.9 us  [the longest x5 0.52 us: factor_column(): lower_cols = jnp.stack(received, 1).reshape(col_tiles, tile_size, tile_size)]
  transfers between devices with their start and end apart: 16 -> 4, of which waited for: 16 -> 3; matrix products, arithmetic and copies ran while one was open for 1% -> 24% of each run, Pallas kernels for 0% -> 0%
where the time goes in v1:
time: 918 us; the launch traced here: 909 us
  waiting for transfers between devices  464 us (51%)
  other arithmetic  197 us (21%)
  matrix products  113 us (12%)
  local copies, waits for them, and re-layouts  107 us (12%)
  between operations  18.4 us (2%)
    all_to_all x1, waiting for transfers between devices, shards(): lax.all_to_all(outgoing, ('row', 'col'), split_axis=0, concat_axis=0, til...  369 us
    another operation x19, other arithmetic, shards(): factor = jnp.tril(jnp.linalg.cholesky(leading))  110 us
    another operation x3, other arithmetic, shards(): lax.linalg.triangular_solve(factor, jnp.eye(panel_order, dtype=jnp.float3...  54.1 us
    all_gather x1, waiting for transfers between devices, shards(): lax.all_gather(panel_rows[:tile_size], 'row', axis=0)[:panel_tiles]  52.2 us
    all_gather x1, waiting for transfers between devices, shards(): panel_rows = lax.all_gather(matrix[:, :, :lead_cols, :], 'col', axis=3)  42.8 us
    dot_general x1, matrix products, shards(): jnp.einsum('trx,xus->trus', lower_tiles, lower_cols.reshape(panel_order,...  28.4 us
    unnamed x27, local copies, waits for them, and re-layouts  26.6 us
    dot_general x1, matrix products, shards(): jnp.einsum('abpq,pqrs->arbs', placement, incoming, precision=highest)  25.3 us
  transfers between devices with their start and end apart: 4, of which 3 were waited for; matrix products, arithmetic and copies ran while one was open for 24% of the time, Pallas kernels for 0%

profile of v1, /device:TPU:0, one launch (start us, length us, event | category | flops | bytes accessed | tf_op | source)
XLA Modules:
  0.0 908.6 jit_solution(637974429758261118)
XLA Ops:
  16.2 5.1 fusion.4
  21.2 24.4 %fusion.2 = f32[32,8,128,128]{3,1,2,0:T(8,128)} fusion(f32[144,128,128]{2,1,0:T(8,128)S(1)} %bitcast.197, f32[144,32,8,1]{0,1,2,3:T(8,128)S(1)} %multiply_bitcast_fusion), kind=kOutput, calls=%fused_computation.10 | convolution fusion | flops 7247757312 | bytes 26361856 | tf_op jit(solution)/shard_map/fpq,frs->pqrs/dot_general | solution.py:77
  45.7 7.5 all-to-all-start
  56.5 369.2 %all-to-all-done = f32[32,8,128,128]{3,1,2,0:T(8,128)} async-done(((f32[32,8,128,128]{3,1,2,0:T(8,128)}), f32[32,8,128,128]{3,1,2,0:T(8,128)}, u32[]{:S(2)}, u32[]{:S(2)}) %all-to-all-start) | async-done | bytes 16777248 | tf_op jit(solution)/shard_map/all_to_all | solution.py:78
  425.7 25.3 %fusion.6 = f32[128,128,12,24]{1,3,2,0:T(8,128)} fusion(f32[12,24,32,8]{1,0,3,2:T(8,128)S(1)} %bitcast.206, f32[32,8,128,128]{3,1,2,0:T(8,128)} %all-to-all-done), kind=kOutput, calls=%fused_computation.15 | convolution fusion | flops 14495514624 | bytes 35946496 | tf_op jit(solution)/shard_map/abpq,pqrs->arbs/dot_general | solution.py:95
  451.0 18.5 %bitcast_add_fusion = f32[12,128,24,128]{3,1,0,2:T(8,128)S(1)} fusion(f32[128,128,12,24]{1,3,2,0:T(8,128)} %fusion.6, f32[12,1,128,24,1,128]{5,4,3,2,1,0:T(1,128)} %param.8), kind=kLoop, calls=%fused_computation.6 | loop fusion | flops 4718592 | bytes 56623104 | tf_op jit(solution)/shard_map/add | solution.py:96
  469.6 6.8 copy-done
  478.1 42.8 %all-gather.8.cloned.1.call-done = f32[12,128,2,512]{3,1,0,2:T(8,128)} async-done(((f32[12,128,2,128]{3,1,0,2:T(8,128)}), f32[12,128,2,512]{3,1,0,2:T(8,128)}) %all-gather.8.cloned.1.call-update) | async-done | bytes 6291472 | tf_op jit(solution)/shard_map/all_gather | solution.py:103
  520.9 7.6 copy.72
  539.2 52.2 %all-gather.10.cloned.1.call-done = f32[1024,640]{0,1:T(8,128)} async-done(((f32[128,640]{0,1:T(8,128)}), f32[1024,640]{0,1:T(8,128)}) %all-gather.10.cloned.1.call-update) | async-done | bytes 2621456 | tf_op jit(solution)/shard_map/all_gather | solution.py:106
  595.6 11.7 %cholesky.133 = f32[128,128]{1,0:T(8,128)S(1)} custom-call(f32[128,128]{1,0:T(8,128)S(1)} %cholesky.340), custom_call_target="Cholesky" | custom-call | tf_op jit(solution)/shard_map/jit(cholesky)/cholesky | solution.py:110
  607.4 9.8 %custom-call.38 = f32[1,128,128]{1,2,0:T(8,128)S(1)} custom-call(f32[1,128,128]{2,1,0:T(8,128)S(1)} %get-tuple-element.63), custom_call_target="InvertDiagBlocksLowerTriangular" | custom-call | tf_op jit(solution)/shard_map/jit(cholesky)/cholesky | solution.py:110
  618.7 13.2 %cholesky.272 = f32[128,128]{1,0:T(8,128)} custom-call(f32[128,128]{1,0:T(8,128)} %cholesky.344), custom_call_target="Cholesky" | custom-call | tf_op jit(solution)/shard_map/jit(cholesky)/cholesky | solution.py:110
  633.3 11.5 %custom-call.39 = f32[1,128,128]{1,2,0:T(8,128)} custom-call(f32[1,128,128]{2,1,0:T(8,128)} %get-tuple-element.60), custom_call_target="InvertDiagBlocksLowerTriangular" | custom-call | tf_op jit(solution)/shard_map/jit(cholesky)/cholesky | solution.py:110
  647.1 12.6 %cholesky.293 = f32[128,128]{1,0:T(8,128)S(1)} custom-call(f32[128,128]{1,0:T(8,128)} %cholesky.349), custom_call_target="Cholesky" | custom-call | tf_op jit(solution)/shard_map/jit(cholesky)/cholesky | solution.py:110
  660.3 10.7 %custom-call.40 = f32[1,128,128]{1,2,0:T(8,128)S(1)} custom-call(f32[1,128,128]{2,1,0:T(8,128)} %get-tuple-element.57), custom_call_target="InvertDiagBlocksLowerTriangular" | custom-call | tf_op jit(solution)/shard_map/jit(cholesky)/cholesky | solution.py:110
  671.7 11.7 %cholesky.312 = f32[128,128]{1,0:T(8,128)S(1)} custom-call(f32[128,128]{1,0:T(8,128)S(1)} %cholesky.354), custom_call_target="Cholesky" | custom-call | tf_op jit(solution)/shard_map/jit(cholesky)/cholesky | solution.py:110
  684.4 9.8 %custom-call.41 = f32[1,128,128]{1,2,0:T(8,128)S(1)} custom-call(f32[1,128,128]{2,1,0:T(8,128)S(1)} %get-tuple-element.54), custom_call_target="InvertDiagBlocksLowerTriangular" | custom-call | tf_op jit(solution)/shard_map/jit(cholesky)/cholesky | solution.py:110
  694.8 11.7 %cholesky.329 = f32[128,128]{1,0:T(8,128)S(1)} custom-call(f32[128,128]{1,0:T(8,128)S(1)} %convolution_subtract_fusion.6), custom_call_target="Cholesky" | custom-call | tf_op jit(solution)/shard_map/jit(cholesky)/cholesky | solution.py:110
  713.3 3.5 fusion.20
  716.9 17.5 %while.3 = (s32[]{:T(128)}, f32[640,640]{1,0:T(8,128)}, s32[5,2]{0,1:T(2,128)S(1)}, f32[5,128,128]{2,1,0:T(8,128)}, s32[]{:T(128)}) while((s32[]{:T(128)}, f32[640,640]{1,0:T(8,128)}, s32[5,2]{0,1:T(2,128)S(1)}, f32[5,128,128]{2,1,0:T(8,128)}, s32[]{:T(128)}) %tuple.49), condition=%wide.while_cond.2, body=%wide.while_body.2.sunk | while | flops 2 | bytes 132205 | solution.py:111
  724.5 2.9 bitcast_dynamic-update-slice_fusion.2
  734.4 50.1 %custom-call.42 = f32[5,128,128]{1,2,0:T(8,128)S(1)} custom-call(f32[5,128,128]{2,1,0:T(8,128)} %get-tuple-element.36), custom_call_target="InvertDiagBlocksLowerTriangular" | custom-call | tf_op jit(solution)/shard_map/triangular_solve | solution.py:111
  794.4 5.8 fusion.12
  805.3 3.2 slice-done
  808.5 4.7 copy.75
  813.2 4.9 copy.110
  818.1 9.1 %copy.76 = f32[3072,640]{1,0:T(8,128)} copy(f32[3072,640]{0,1:T(8,128)} %bitcast.200) | data formatting | bytes 15728640 | tf_op jit(solution)/shard_map/yx,xc->yc/dot_general | solution.py:115
  827.3 13.6 %fusion.17 = f32[640,24,128]{2,0,1:T(8,128)} fusion(f32[24,128,640]{2,1,0:T(8,128)} %bitcast.198, f32[640,640]{1,0:T(8,128)} %copy-done.6), kind=kOutput, calls=%fused_computation.32 | convolution fusion | flops 7549747200 | bytes 17367040 | tf_op jit(solution)/shard_map/yx,xc->yc/dot_general | solution.py:115
  840.9 28.4 %subtract_select_fusion = f32[12,128,24,128]{3,1,0,2:T(8,128)S(1)} fusion(f32[12,128,24,128]{3,1,0,2:T(8,128)} %copy-done, pred[12]{0:T(512)(128)(4,1)S(1)} %add_compare_fusion.2, f32[640,24,128]{2,0,1:T(8,128)} %fusion.17, f32[12,128,640]{2,1,0:T(8,128)S(1)} %bitcast.196), kind=kOutput, calls=%fused_computation.7 | convolution fusion | flops 18129813504 | bytes 49545228 | tf_op jit(solution)/shard_map/trx,xus->trus/dot_general | solution.py:118
  870.6 7.5 copy.131
  879.1 22.5 %copy.79 = f32[12,1,128,24,1,128]{5,4,3,2,1,0:T(1,128)} copy(f32[12,1,128,24,1,128]{5,2,0,3,4,1:T(8,128)} %fusion.42) | data formatting | bytes 37748736 | tf_op jit(solution)/shard_map/scatter | solution.py:135
  (146 shorter events, 72.0 us)
Async XLA Ops:
  45.7 380.1 %all-to-all-start = ((f32[32,8,128,128]{3,1,2,0:T(8,128)}), f32[32,8,128,128]{3,1,2,0:T(8,128)}, u32[]{:S(2)}, u32[]{:S(2)}) async-start(f32[32,8,128,128]{3,1,2,0:T(8,128)} %fusion.2), calls=%async_computation | async-start | bytes 33554432 | tf_op jit(solution)/shard_map/all_to_all | solution.py:78
  53.1 467.8 %all-gather.8.cloned.1.call-start = ((), (), s32[]{:S(2)}) async-start(), calls=%async_computation.2 | async-start | bytes 7864320 | tf_op jit(solution)/shard_map/all_gather | solution.py:103
  469.5 6.9 copy-start
  477.7 113.7 %all-gather.10.cloned.1.call-start = ((), (), s32[]{:S(2)}) async-start(), calls=%async_computation.3 | async-start | bytes 2949120 | tf_op jit(solution)/shard_map/all_gather | solution.py:106
  530.1 2.6 copy-start.4
  533.6 271.6 %all-gather.6.cloned.1.call-start = ((), (), s32[]{:S(2)}) async-start(), calls=%async_computation.1 | async-start | bytes 14155776 | tf_op jit(solution)/shard_map/all_gather | solution.py:108
  591.4 1.4 slice-start.3
  711.9 1.4 copy-start.5
  713.3 3.5 copy-start.8
  713.3 81.1 %slice-start.1 = ((s8[6291456]{0:T(1024)(128)(4,1)}), s8[2097152]{0:T(1024)(128)(4,1)S(1)}, s32[]{:S(2)}) async-start(s8[6291456]{0:T(1024)(128)(4,1)} %bitcast.202), calls=%async_computation.5 | async-start | bytes 4194304
  784.5 3.2 copy-start.7
  787.7 6.7 slice-start.2
  794.4 5.8 copy-start.6
  800.3 1.9 copy-start.1
  805.3 3.2 slice-start
  827.2 13.7 %copy-start.2 = (f32[1536,640]{1,0:T(8,128)S(1)}, f32[1536,640]{1,0:T(8,128)}, u32[]{:S(2)}) copy-start(f32[1536,640]{1,0:T(8,128)} %copy-done.1) | copy-start | bytes 11796484
  870.6 7.5 copy-start.3
Sparse Core Ops, SparseCore 0:
  477.8 43.0 all-gather.7
  533.8 57.5 all-gather.9
  593.6 174.1 all-gather.5

commit v2 on v1

--- a/solution.py
+++ b/solution.py
@@ -1,6 +1,9 @@
+import functools
 import jax
 import jax.numpy as jnp
 from jax import lax
+from jax.experimental import pallas as pl
+from jax.experimental.pallas import tpu as pltpu
 from jax.sharding import PartitionSpec as P
 
 PT = 5
@@ -20,6 +23,57 @@
 
 def one_hot(values, length):
     return (values[..., None] == jnp.arange(length, dtype=jnp.int32)).astype(jnp.float32)
+
+
+def split(value, axis, second):
+    rounded = lax.reduce_precision(value, 8, 7)
+    large = rounded.astype(jnp.bfloat16)
+    small = (value - rounded).astype(jnp.bfloat16)
+    return jnp.concatenate([large, small, large] if second else [large, large, small], axis)
+
+
+def update_kernel(panel_tiles, rows_count, cols_count, ids, m_ref, l_ref, c_ref, p_ref, o_ref):
+    block, tile_size, col_tiles, _ = m_ref.shape
+    lead_cols = p_ref.shape[0]
+    lhs = l_ref[...].reshape(block * tile_size, l_ref.shape[2])
+    local = lax.broadcasted_iota(jnp.int32, (block, tile_size, tile_size), 0)
+    glob = (local + pl.program_id(0) * block) * rows_count + ids[0]
+    for pair in range(col_tiles // 2):
+        product = jnp.dot(
+            lhs,
+            c_ref[:, pair * 2 * tile_size : (pair + 1) * 2 * tile_size],
+            preferred_element_type=jnp.float32,
+        )
+        for half in range(2):
+            column = 2 * pair + half
+            part = product[:, half * tile_size : (half + 1) * tile_size]
+            tiles = m_ref[:, :, column, :] - part.reshape(block, tile_size, tile_size)
+            tiles = jnp.where(glob >= panel_tiles, tiles, 0.0)
+            if column < lead_cols:
+                inside = column * cols_count + ids[1] < panel_tiles
+                tiles = jnp.where(inside, p_ref[column], tiles)
+            o_ref[:, :, column, :] = tiles
+
+
+def update(ids, matrix, lower_tiles, lower_cols, panel, panel_tiles, rows_count, cols_count):
+    row_tiles, tile_size, col_tiles, _ = matrix.shape
+    depth = lower_tiles.shape[2]
+    block = next(size for size in (4, 3, 2, 1) if row_tiles % size == 0)
+    matrix_spec = pl.BlockSpec((block, tile_size, col_tiles, tile_size), lambda i: (i, 0, 0, 0))
+    return pl.pallas_call(
+        functools.partial(update_kernel, panel_tiles, rows_count, cols_count),
+        grid=(row_tiles // block,),
+        in_specs=[
+            pl.BlockSpec(memory_space=pltpu.SMEM),
+            matrix_spec,
+            pl.BlockSpec((block, tile_size, depth), lambda i: (i, 0, 0)),
+            pl.BlockSpec(lower_cols.shape, lambda i: (0, 0), pipeline_mode=pl.Buffered(1)),
+            pl.BlockSpec((panel.shape[0], block, tile_size, tile_size), lambda i: (0, i, 0, 0)),
+        ],
+        out_specs=matrix_spec,
+        out_shape=jax.ShapeDtypeStruct(matrix.shape, jnp.float32),
+        compiler_params=pltpu.CompilerParams(vmem_limit_bytes=60 * 1024 * 1024),
+    )(ids, matrix, lower_tiles, lower_cols, panel)
 
 
 def shards(front, child_updates, child_maps, child_orders):
@@ -32,6 +86,27 @@
     col_id = lax.axis_index("col")
     matrix = front.reshape(row_tiles, tile_size, col_tiles, tile_size)
     pieces = child_updates.reshape(child_rows, tile_size, child_cols, tile_size)
+    panel_tiles = PANELS * PT
+    panel_order = panel_tiles * tile_size
+    lead_cols = -(-panel_tiles // cols_count)
+    high = lax.Precision.HIGH
+    panel_range = jnp.arange(panel_tiles, dtype=jnp.int32)
+
+    def place_row(tile_row, tiles):
+        return jnp.where((panel_range == tile_row)[:, None, None, None], tiles[None], 0.0)
+
+    lead = place_row(row_id, matrix[0, :, :lead_cols, :])
+    for index in range(-(-panel_tiles // half_rows)):
+        child_row = index * half_rows + row_id % half_rows
+        lead = lead + place_row(child_row, pieces[index, :, :lead_cols, :])
+    col_range = jnp.arange(cols_count, dtype=jnp.int32)
+    lead = jnp.where((col_range == col_id)[:, None], lead[:, :, :, None, :], 0.0)
+    lead = lead.reshape(panel_order, lead_cols * cols_count * tile_size)[:, :panel_order]
+    leading = lax.psum(lead, ("row", "col"))
+    factor = jnp.tril(jnp.linalg.cholesky(leading))
+    inverse = lax.linalg.triangular_solve(
+        factor, jnp.eye(panel_order, dtype=jnp.float32), left_side=True, lower=True
+    )
     cap_rows = max(1, 2 * RUN // rows_count)
     cap_cols = max(1, RUN // cols_count) ** 2
     sources = jnp.arange(rows_count, dtype=jnp.int32)
@@ -76,6 +151,7 @@
     flat_pieces = pieces.transpose(0, 2, 1, 3).reshape(tile_count, tile_size, tile_size)
     outgoing = jnp.einsum("fpq,frs->pqrs", send_tiles, flat_pieces, precision=highest)
     incoming = lax.all_to_all(outgoing, ("row", "col"), split_axis=0, concat_axis=0, tiled=True)
+    incoming, inverse = lax.optimization_barrier((incoming, inverse))
     arrive_tiles = (tile_dest == row_id * cols_count + col_id).astype(jnp.float32)
     row_slot_flat = jnp.broadcast_to(
         slot_rows[:, None, :, None], (rows_count, cols_count, child_rows, child_cols)
@@ -96,45 +172,33 @@
     matrix = matrix + added
     glob_rows = jnp.arange(row_tiles, dtype=jnp.int32) * rows_count + row_id
 
-    panel_tiles = PANELS * PT
-    panel_order = panel_tiles * tile_size
-    lead_cols = -(-panel_tiles // cols_count)
-    high = lax.Precision.HIGH
+    panel_cols = lax.all_gather(matrix[0], "row", axis=0)[:panel_tiles]
+    panel_cols = panel_cols.reshape(panel_order, col_tiles * tile_size)
     panel_rows = lax.all_gather(matrix[:, :, :lead_cols, :], "col", axis=3)
     panel_rows = panel_rows.reshape(row_tiles * tile_size, lead_cols * cols_count * tile_size)
     panel_rows = panel_rows[:, :panel_order]
-    leading = lax.all_gather(panel_rows[:tile_size], "row", axis=0)[:panel_tiles]
-    leading = leading.reshape(panel_order, panel_order)
-    panel_cols = lax.all_gather(matrix[0], "row", axis=0)[:panel_tiles]
-    panel_cols = panel_cols.reshape(panel_order, col_tiles * tile_size)
-    factor = jnp.tril(jnp.linalg.cholesky(leading))
-    inverse = lax.linalg.triangular_solve(
-        factor, jnp.eye(panel_order, dtype=jnp.float32), left_side=True, lower=True
-    )
     lower_rows = jnp.einsum("rx,yx->ry", panel_rows, inverse, precision=high)
     lower_cols = jnp.einsum("yx,xc->yc", inverse, panel_cols, precision=high)
-    below = (glob_rows >= panel_tiles)[:, None, None]
-    lower_tiles = jnp.where(below, lower_rows.reshape(row_tiles, tile_size, panel_order), 0.0)
-    update = jnp.einsum(
-        "trx,xus->trus",
-        lower_tiles,
-        lower_cols.reshape(panel_order, col_tiles, tile_size),
-        precision=high,
-    )
-    matrix = jnp.where(below[..., None], matrix - update, 0.0)
+    lower_tiles = lower_rows.reshape(row_tiles, tile_size, panel_order)
     factor_row = lax.dynamic_slice_in_dim(
         factor, jnp.minimum(row_id, panel_tiles - 1) * tile_size, tile_size, 0
     )
     top = jnp.where(row_id < panel_tiles, factor_row, lower_tiles[0])
     panel = jnp.concatenate([top[None], lower_tiles[1:]], 0)
+    columns = []
     for local_col in range(lead_cols):
-        column = local_col * cols_count + col_id
-        piece = lax.dynamic_slice_in_dim(
-            panel, jnp.minimum(column, panel_tiles - 1) * tile_size, tile_size, 2
-        )
-        matrix = matrix.at[:, :, local_col, :].set(
-            jnp.where(column < panel_tiles, piece, matrix[:, :, local_col, :])
-        )
+        column = jnp.minimum(local_col * cols_count + col_id, panel_tiles - 1)
+        columns.append(lax.dynamic_slice_in_dim(panel, column * tile_size, tile_size, 2))
+    matrix = update(
+        jnp.stack([row_id, col_id]).astype(jnp.int32),
+        matrix,
+        split(lower_tiles, 2, False),
+        split(lower_cols, 0, True),
+        jnp.stack(columns, 0),
+        panel_tiles,
+        rows_count,
+        cols_count,
+    )
     return matrix.reshape(row_tiles, 1, tile_size, col_tiles, 1, tile_size)
 
 

time: 918 us -> 938 us (1.022)
  Pallas kernels: 0 us -> 47.4 us
  local copies, waits for them, and re-layouts: 107 us -> 60.4 us
  waiting for transfers between devices: 464 us -> 508 us
  matrix products: 113 us -> 92.1 us
    all_to_all x1, waiting for transfers between devices: 369 us -> 0.01 us  [shards(): lax.all_to_all(outgoing, ('row', 'col'), split_axis=0, concat_axis=0, til...]
    psum x0 -> x1, waiting for transfers between devices: none -> 300 us  [shards(): leading = lax.psum(lead, ('row', 'col'))]
    all_gather x1, waiting for transfers between devices: 0.02 us -> 160 us  [shards(): panel_cols = lax.all_gather(matrix[0], 'row', axis=0)[:panel_tiles]]
    all_gather x1 -> x0, waiting for transfers between devices: 52.2 us -> none  [shards(): lax.all_gather(panel_rows[:tile_size], 'row', axis=0)[:panel_tiles]]
    pallas_call x0 -> x1, Pallas kernels: none -> 47.4 us  [update(): pl.pallas_call(functools.partial(update_kernel, panel_tiles, rows_count,...]
    dot_general x1 -> x0, matrix products: 28.4 us -> none  [shards(): jnp.einsum('trx,xus->trus', lower_tiles, lower_cols.reshape(panel_order,...]
    scatter x1 -> x0, local copies, waits for them, and re-layouts: 22.5 us -> none  [shards(): matrix.at[:, :, local_col, :]]
    add x1, other arithmetic: 18.5 us -> 0.49 us  [shards(): lead = lead + place_row(child_row, pieces[index, :, :lead_cols, :])]
  transfers between devices with their start and end apart: 4 -> 4, of which waited for: 3 -> 3; matrix products, arithmetic and copies ran while one was open for 24% -> 27% of each run, Pallas kernels for 0% -> 0%
where the time goes in v2:
time: 938 us; the launch traced here: 929 us
  waiting for transfers between devices  508 us (54%)
  other arithmetic  194 us (21%)
  matrix products  92.1 us (10%)
  local copies, waits for them, and re-layouts  60.4 us (6%)
  Pallas kernels  47.4 us (5%)
  between operations  18.8 us (2%)
    psum x1, waiting for transfers between devices, shards(): leading = lax.psum(lead, ('row', 'col'))  300 us
    all_gather x1, waiting for transfers between devices, shards(): panel_cols = lax.all_gather(matrix[0], 'row', axis=0)[:panel_tiles]  160 us
    another operation x19, other arithmetic, shards(): factor = jnp.tril(jnp.linalg.cholesky(leading))  117 us
    another operation x3, other arithmetic, shards(): lax.linalg.triangular_solve(factor, jnp.eye(panel_order, dtype=jnp.float3...  52.8 us
    all_gather x1, waiting for transfers between devices, shards(): panel_rows = lax.all_gather(matrix[:, :, :lead_cols, :], 'col', axis=3)  47.6 us
    pallas_call x1, Pallas kernels, update(): pl.pallas_call(functools.partial(update_kernel, panel_tiles, rows_count,...  47.4 us
    dot_general x1, matrix products, shards(): jnp.einsum('abpq,pqrs->arbs', placement, incoming, precision=highest)  27 us
    dot_general x1, matrix products, shards(): jnp.einsum('fpq,frs->pqrs', send_tiles, flat_pieces, precision=highest)  24.2 us
  transfers between devices with their start and end apart: 4, of which 3 were waited for; matrix products, arithmetic and copies ran while one was open for 27% of the time, Pallas kernels for 0%

profile of v2, /device:TPU:0, one launch (start us, length us, event | category | flops | bytes accessed | tf_op | source)
XLA Modules:
  0.0 928.6 jit_solution(3728039921960496144)
XLA Ops:
  16.1 5.1 multiply_multiply_fusion
  21.2 24.2 %fusion.3 = f32[32,8,128,128]{3,1,2,0:T(8,128)} fusion(f32[144,128,128]{2,1,0:T(8,128)S(1)} %bitcast.180, f32[144,8]{0,1:T(8,128)S(1)} %fusion.81, f32[144,32]{0,1:T(8,128)S(1)} %fusion.80), kind=kOutput, calls=%fused_computation.13 | convolution fusion | flops 7247794176 | bytes 26237440 | tf_op jit(solution)/shard_map/fpq,frs->pqrs/dot_general | solution.py:152
  45.5 7.5 all-to-all-start
  53.0 8.8 copy.97
  75.2 3.6 fusion.12
  78.9 299.8 %all-reduce.3.cloned.1.call-done = f32[640,640]{0,1:T(8,128)} async-done(((f32[640,640]{0,1:T(8,128)}), f32[640,640]{0,1:T(8,128)}) %all-reduce.3.cloned.1.call-update) | async-done | bytes 1638416 | tf_op jit(solution)/shard_map/psum | solution.py:105
  382.3 11.7 %cholesky.133 = f32[128,128]{1,0:T(8,128)S(1)} custom-call(f32[128,128]{1,0:T(8,128)S(1)} %cholesky.340), custom_call_target="Cholesky" | custom-call | tf_op jit(solution)/shard_map/jit(cholesky)/cholesky | solution.py:106
  394.0 9.8 %custom-call.38 = f32[1,128,128]{1,2,0:T(8,128)S(1)} custom-call(f32[1,128,128]{2,1,0:T(8,128)S(1)} %get-tuple-element.51), custom_call_target="InvertDiagBlocksLowerTriangular" | custom-call | tf_op jit(solution)/shard_map/jit(cholesky)/cholesky | solution.py:106
  405.3 13.2 %cholesky.272 = f32[128,128]{1,0:T(8,128)} custom-call(f32[128,128]{1,0:T(8,128)} %cholesky.344), custom_call_target="Cholesky" | custom-call | tf_op jit(solution)/shard_map/jit(cholesky)/cholesky | solution.py:106
  420.0 20.0 %custom-call.39 = f32[1,128,128]{1,2,0:T(8,128)} custom-call(f32[1,128,128]{2,1,0:T(8,128)} %get-tuple-element.48), custom_call_target="InvertDiagBlocksLowerTriangular" | custom-call | tf_op jit(solution)/shard_map/jit(cholesky)/cholesky | solution.py:106
  442.2 12.5 %cholesky.293 = f32[128,128]{1,0:T(8,128)S(1)} custom-call(f32[128,128]{1,0:T(8,128)} %cholesky.349), custom_call_target="Cholesky" | custom-call | tf_op jit(solution)/shard_map/jit(cholesky)/cholesky | solution.py:106
  455.4 10.6 %custom-call.40 = f32[1,128,128]{1,2,0:T(8,128)S(1)} custom-call(f32[1,128,128]{2,1,0:T(8,128)} %get-tuple-element.45), custom_call_target="InvertDiagBlocksLowerTriangular" | custom-call | tf_op jit(solution)/shard_map/jit(cholesky)/cholesky | solution.py:106
  466.8 11.9 %cholesky.312 = f32[128,128]{1,0:T(8,128)S(1)} custom-call(f32[128,128]{1,0:T(8,128)S(1)} %cholesky.354), custom_call_target="Cholesky" | custom-call | tf_op jit(solution)/shard_map/jit(cholesky)/cholesky | solution.py:106
  478.8 9.8 %custom-call.41 = f32[1,128,128]{1,2,0:T(8,128)S(1)} custom-call(f32[1,128,128]{2,1,0:T(8,128)S(1)} %get-tuple-element.42), custom_call_target="InvertDiagBlocksLowerTriangular" | custom-call | tf_op jit(solution)/shard_map/jit(cholesky)/cholesky | solution.py:106
  489.2 11.7 %cholesky.329 = f32[128,128]{1,0:T(8,128)S(1)} custom-call(f32[128,128]{1,0:T(8,128)S(1)} %convolution_subtract_fusion.6), custom_call_target="Cholesky" | custom-call | tf_op jit(solution)/shard_map/jit(cholesky)/cholesky | solution.py:106
  509.9 17.9 %while.1 = (s32[]{:T(128)}, f32[640,640]{1,0:T(8,128)}, s32[5,2]{0,1:T(2,128)S(1)}, f32[5,128,128]{2,1,0:T(8,128)}, s32[]{:T(128)}) while((s32[]{:T(128)}, f32[640,640]{1,0:T(8,128)}, s32[5,2]{0,1:T(2,128)S(1)}, f32[5,128,128]{2,1,0:T(8,128)}, s32[]{:T(128)}) %tuple.48), condition=%wide.while_cond, body=%wide.while_body.sunk | while | flops 2 | bytes 132205 | solution.py:107
  510.5 2.9 bitcast_dynamic-update-slice_fusion.2
  514.1 2.9 bitcast_dynamic-update-slice_fusion.2
  517.7 2.9 bitcast_dynamic-update-slice_fusion.2
  521.3 2.9 bitcast_dynamic-update-slice_fusion.2
  527.8 50.3 %custom-call.42 = f32[5,128,128]{1,2,0:T(8,128)S(1)} custom-call(f32[5,128,128]{2,1,0:T(8,128)} %get-tuple-element.16), custom_call_target="InvertDiagBlocksLowerTriangular" | custom-call | tf_op jit(solution)/shard_map/triangular_solve | solution.py:107
  592.4 27.0 %bitcast_add_fusion.m_ref = f32[12,128,24,128]{3,2,1,0:T(8,128)} fusion(f32[12,128,24,128]{3,2,1,0:T(8,128)} %bitcast.183, f32[32,8,128,128]{3,1,2,0:T(8,128)} %all-to-all-done, f32[12,24,32,8,1]{1,0,3,2,4:T(8,128)S(1)} %bitcast.187), kind=kOutput, calls=%fused_computation.6 | convolution fusion | flops 14500233216 | bytes 54820864 | tf_op jit(solution)/shard_map/abpq,pqrs->arbs/dot_general | solution.py:171
  619.3 4.4 slice.218
  627.4 47.6 %all-gather.6.cloned.1.call-done = f32[12,128,2,512]{3,2,1,0:T(2,128)} async-done(((f32[12,128,2,128]{3,2,1,0:T(2,128)}), f32[12,128,2,512]{3,2,1,0:T(2,128)}) %all-gather.6.cloned.1.call-update) | async-done | bytes 6291472 | tf_op jit(solution)/shard_map/all_gather | solution.py:177
  675.0 4.3 copy.74
  679.3 7.3 fusion.15
  690.1 3.0 pad_maximum_fusion.1.l_ref
  693.1 160.2 %all-gather.4.cloned.1.call-done = f32[8,128,24,128]{3,2,1,0:T(8,128)} async-done(((f32[1,128,24,128]{3,2,1,0:T(8,128)}), f32[8,128,24,128]{3,2,1,0:T(8,128)}) %all-gather.4.cloned.1.call-update) | async-done | bytes 12582928 | tf_op jit(solution)/shard_map/all_gather | solution.py:175
  853.3 3.2 slice-done
  856.6 12.1 %fusion.8 = (bf16[640,3072]{1,0:T(8,128)(2,1)S(1)}, bf16[640,3072]{1,0:T(8,128)(2,1)S(1)}) fusion(f32[640,640]{1,0:T(8,128)} %convolution_dynamic-update-slice_fusion, f32[80,8,24,128]{3,2,1,0:T(8,128)S(1)} %bitcast.186), kind=kOutput, calls=%fused_computation.18 | convolution fusion | flops 7557611520 | bytes 17367040 | tf_op jit(solution)/shard_map/yx,xc->yc/dot_general | solution.py:181
  868.7 5.6 pad_maximum_fusion.c_ref
  874.3 47.4 %shard_map.46 = f32[12,128,24,128]{3,2,1,0:T(8,128)} custom-call(s32[2]{0:T(128)} %pad_add_fusion.ids, f32[12,128,24,128]{3,2,1,0:T(8,128)} %bitcast_add_fusion.m_ref, bf16[12,128,1920]{2,1,0:T(8,128)(2,1)} %pad_maximum_fusion.1.l_ref, bf16[1920,3072]{1,0:T(8,128)(2,1)} %pad_maximum_fusion.c_ref, f32[2,12,128,128]{3,2,1,0:T(8,128)} %pad_maximum_fusion.2.p_ref), custom_call_target="tpu_custom_call" | custom-call | tf_op jit(solution)/shard_map/pallas_call | solution.py:63
  (142 shorter events, 65.4 us)
Async XLA Ops:
  45.5 546.9 %all-to-all-start = ((f32[32,8,128,128]{3,1,2,0:T(8,128)}), f32[32,8,128,128]{3,1,2,0:T(8,128)}, u32[]{:S(2)}, u32[]{:S(2)}) async-start(f32[32,8,128,128]{3,1,2,0:T(8,128)} %fusion.3), calls=%async_computation | async-start | bytes 33554432 | tf_op jit(solution)/shard_map/all_to_all | solution.py:153
  52.9 325.8 %all-reduce.3.cloned.1.call-start = ((), (), s32[]{:S(2)}) async-start(), calls=%async_computation.1 | async-start | bytes 3276800 | tf_op jit(solution)/shard_map/psum | solution.py:105
  67.2 1.4 slice-start.1
  71.1 603.9 %all-gather.6.cloned.1.call-start = ((), (), s32[]{:S(2)}) async-start(), calls=%async_computation.3 | async-start | bytes 7864320 | tf_op jit(solution)/shard_map/all_gather | solution.py:177
  378.7 2.2 copy-start
  381.1 1.2 copy-start.2
  382.3 21.7 %copy-start.3 = (f32[640,640]{1,0:T(8,128)S(1)}, f32[640,640]{1,0:T(8,128)}, u32[]{:S(2)}) copy-start(f32[640,640]{1,0:T(8,128)} %copy-done.2) | copy-start | bytes 4915204
  507.9 1.9 copy-start.6
  507.9 72.2 %copy-start.4 = (f32[640,640]{1,0:T(8,128)S(1)}, f32[640,640]{1,0:T(8,128)}, u32[]{:S(2)}) copy-start(f32[640,640]{1,0:T(8,128)} %fusion.48) | copy-start | bytes 4915204
  578.1 8.9 copy-start.5
  588.2 4.2 copy-start.1
  623.7 229.6 %all-gather.4.cloned.1.call-start = ((), (), s32[]{:S(2)}) async-start(), calls=%async_computation.2 | async-start | bytes 14155776 | tf_op jit(solution)/shard_map/all_gather | solution.py:175
  853.3 3.2 slice-start
Sparse Core Ops, SparseCore 0:
  71.3 307.3 all-reduce.2
  623.9 51.0 all-gather.5
  677.2 176.0 all-gather.3
